TPU v7x, 32 devices: a whole 2x2x4 slice. The times are simulated.
32 devices in a mesh: tile: 8 (over y, x, core), depth: 4 (over z).
Axes of the slice: x: 2, y: 2, z: 4, core: 2. Of those that a mesh axis runs over, the one named last changes fastest.
Arguments:
- initial_state: float32 [2, 32, 8192], P(None, 'depth', 'tile'), may hold values from -6 to 6
- observed: float32 [2, 32, 8192], P(None, 'depth', 'tile'), may hold values from -6 to 6
- edge_weight: float32 [8192], P('tile'), may hold values from 0.25 to 1
- land: int32 [8192], P('tile'), may hold values 0 or 1
- w_in: bfloat16 [64, 640], replicated, may hold values from -0.75 to 0.75
- b_in: float32 [640], replicated, may hold values from -3 to 3
- w_mid: bfloat16 [640, 640], replicated, may hold values from -0.25 to 0.25
- b_mid: float32 [640], replicated, may hold values from -3 to 3
- w_out: bfloat16 [640, 64], replicated, may hold values from -0.25 to 0.25
- b_out: float32 [64], replicated, may hold values from -3 to 3
Outputs:
- final_state: float32 [2, 32, 8192], P(None, 'depth', 'tile')
- sensitivity: float32 [2, 32, 8192], P(None, 'depth', 'tile')
- grad_w_in: float32 [64, 640], replicated
- grad_b_in: float32 [640], replicated
- grad_w_mid: float32 [640, 640], replicated
- grad_b_mid: float32 [640], replicated
- grad_w_out: float32 [640, 64], replicated
- grad_b_out: float32 [64], replicated
All inputs are finite; a program needn't handle non-finite values. No bound on the sum of `land` on one device may be relied on, other than what follows from the above.
Results may differ from a plain program's by a relative error of at most 0.0017.
Values may be sent and summed in bfloat16 or wider, within the bound.
No kernel may reach another device: no remote copies, remote signals or barrier semaphores. Data moves between devices by JAX's collectives and lax.ppermute only.
A program may use at most 64 MiB of HBM per device.

v0:
```python
import jax
import jax.numpy as jnp
from jax import lax
from jax.sharding import PartitionSpec as P

TILE_SIDE = 32
LEVELS = 32
TIME_STEPS = 2
FEATURES = 64
TILE_CELLS = 1024
diffuse_coef = 0.2
step_size = 0.5


def with_halo(cells, sides, width):
    for axis, dim in sides:
        count = lax.axis_size(axis)
        head = lax.slice_in_dim(cells, 0, width, axis=dim)
        tail = lax.slice_in_dim(cells, cells.shape[dim] - width, cells.shape[dim], axis=dim)
        cells = jnp.concatenate(
            [
                lax.ppermute(tail, axis, [(i, (i + 1) % count) for i in range(count)]),
                cells,
                lax.ppermute(head, axis, [((i + 1) % count, i) for i in range(count)]),
            ],
            axis=dim,
        )
    return cells


def passed_along(x, axis, by):
    length = lax.axis_size(axis)
    return lax.ppermute(x, axis, [(i, (i + by) % length) for i in range(length)])


def neighbour_sum(flat_rows):
    row_count = flat_rows.shape[0]
    tile_grid = flat_rows.reshape(row_count, TILE_SIDE, TILE_SIDE)
    zonal_pair = jnp.stack([tile_grid[:, :, -1], tile_grid[:, :, 0]], axis=1)
    padded = with_halo(zonal_pair[None], (("tile", 0),), 1)
    from_west = padded[0, :, 0, :]
    from_east = padded[2, :, 1, :]
    fold_pair = jnp.stack([tile_grid[:, 0, :], tile_grid[:, -1, :]], axis=1)
    across = passed_along(fold_pair, "tile", lax.axis_size("tile") // 2)[:, :, ::-1]
    west_cells = jnp.concatenate([from_west[:, :, None], tile_grid[:, :, :-1]], axis=2)
    east_cells = jnp.concatenate([tile_grid[:, :, 1:], from_east[:, :, None]], axis=2)
    south_cells = jnp.concatenate([across[:, 0, None, :], tile_grid[:, :-1, :]], axis=1)
    north_cells = jnp.concatenate([tile_grid[:, 1:, :], across[:, 1, None, :]], axis=1)
    return (west_cells + east_cells + south_cells + north_cells).reshape(row_count, TILE_CELLS)


def diffuse(tracer_field, weight, weight_sums):
    flat_rows = tracer_field.reshape(-1, TILE_CELLS)
    scaled = flat_rows * weight[None, :]
    result_rows = weight[None, :] * (neighbour_sum(scaled) - flat_rows * weight_sums[None, :])
    return result_rows.reshape(tracer_field.shape)


def silu_slope(pre_act):
    sigmoid_val = jax.nn.sigmoid(pre_act)
    return sigmoid_val * (1.0 + pre_act * (1.0 - sigmoid_val))


def closure_forward(inputs, params):
    w_in, b_in, w_mid, b_mid, w_out, b_out = params
    contract_rows = (((0,), (0,)), ((), ()))
    pre_one = (
        lax.dot_general(w_in, inputs, contract_rows, preferred_element_type=jnp.float32)
        + b_in[:, None]
    )
    hidden_one = jax.nn.silu(pre_one).astype(jnp.bfloat16)
    pre_two = (
        lax.dot_general(w_mid, hidden_one, contract_rows, preferred_element_type=jnp.float32)
        + b_mid[:, None]
    )
    hidden_two = jax.nn.silu(pre_two).astype(jnp.bfloat16)
    output = (
        lax.dot_general(w_out, hidden_two, contract_rows, preferred_element_type=jnp.float32)
        + b_out[:, None]
    )
    return (output, (inputs, pre_one, hidden_one, pre_two, hidden_two))


def closure_backward(upstream, saved_cache, params):
    w_in, b_in, w_mid, b_mid, w_out, b_out = params
    inputs, pre_one, hidden_one, pre_two, hidden_two = saved_cache
    contract_cols = (((1,), (1,)), ((), ()))
    grad_w_out = lax.dot_general(
        hidden_two, upstream, contract_cols, preferred_element_type=jnp.float32
    )
    grad_b_out = jnp.sum(upstream.astype(jnp.float32), axis=1)
    slope_two = (
        jnp.dot(w_out, upstream, preferred_element_type=jnp.float32) * silu_slope(pre_two)
    ).astype(jnp.bfloat16)
    grad_w_mid = lax.dot_general(
        hidden_one, slope_two, contract_cols, preferred_element_type=jnp.float32
    )
    grad_b_mid = jnp.sum(slope_two.astype(jnp.float32), axis=1)
    slope_one = (
        jnp.dot(w_mid, slope_two, preferred_element_type=jnp.float32) * silu_slope(pre_one)
    ).astype(jnp.bfloat16)
    grad_w_in = lax.dot_general(
        inputs, slope_one, contract_cols, preferred_element_type=jnp.float32
    )
    grad_b_in = jnp.sum(slope_one.astype(jnp.float32), axis=1)
    back_grad = jnp.dot(w_in, slope_one, preferred_element_type=jnp.float32)
    return (back_grad, (grad_w_in, grad_b_in, grad_w_mid, grad_b_mid, grad_w_out, grad_b_out))


def is_power_of_two(count):
    return count & count - 1 == 0


def swapped(x, axis, even_bit, odd_bit):
    length = lax.axis_size(axis)
    return lax.ppermute(x, axis, [(i, i ^ (odd_bit if i & 1 else even_bit)) for i in range(length)])


def tile_rounds(length):
    bits = [1 << k for k in range(length.bit_length() - 1)]
    rounds = [(bits[0], bits[0])] if bits else []
    rest = bits[1:]
    for k in range(len(rest)):
        rounds.append((rest[k], rest[(k + 1) % len(rest)]))
    return rounds


def all_summed(block):
    tiles = lax.axis_size("tile")
    depths = lax.axis_size("depth")
    if not (is_power_of_two(tiles) and is_power_of_two(depths)):
        return lax.psum(block, ("tile", "depth"))
    width = block.shape[-1]
    tile = lax.axis_index("tile")
    rounds = tile_rounds(tiles)
    sides = []
    for even_bit, odd_bit in rounds:
        bit = jnp.where(tile & 1 == 1, odd_bit, even_bit)
        sides.append((tile & bit != 0).astype(jnp.int32))
    for (even_bit, odd_bit), side in zip(rounds, sides):
        halves = block.reshape(2, -1, width)
        sent = lax.dynamic_index_in_dim(halves, 1 - side, 0, False)
        kept = lax.dynamic_index_in_dim(halves, side, 0, False)
        block = kept + swapped(sent, "tile", even_bit, odd_bit)
    bit = 1
    while bit < depths:
        block = block + swapped(block, "depth", bit, bit)
        bit *= 2
    for (even_bit, odd_bit), side in zip(reversed(rounds), reversed(sides)):
        other = swapped(block, "tile", even_bit, odd_bit)
        block = jnp.where(side == 0, jnp.stack([block, other]), jnp.stack([other, block])).reshape(
            -1, width
        )
    return block


def reduced_gradients(totals):
    grad_w_in, grad_b_in, grad_w_mid, grad_b_mid, grad_w_out, grad_b_out = totals
    width = grad_w_mid.shape[1]
    features = grad_w_in.shape[0]
    bias_rows = jnp.zeros((8, width), jnp.float32)
    bias_rows = (
        bias_rows.at[0].set(grad_b_in).at[1].set(grad_b_mid).at[2, :features].set(grad_b_out)
    )
    parts = [grad_w_mid, grad_w_in, grad_w_out.T, bias_rows]
    rows = sum((part.shape[0] for part in parts))
    step = 8 * lax.axis_size("tile")
    pad = -rows % step
    block = jnp.concatenate(parts + [jnp.zeros((pad, width), jnp.float32)], axis=0)
    block = all_summed(block)
    top = width
    out_in = block[top : top + features]
    out_out = block[top + features : top + 2 * features].T
    biases = block[top + 2 * features : top + 2 * features + 8]
    return (out_in, biases[0], block[:width], biases[1], out_out, biases[2, :features])


def body(initial_state, observed, edge_weight, land, w_in, b_in, w_mid, b_mid, w_out, b_out):
    params = (w_in, b_in, w_mid, b_mid, w_out, b_out)
    ocean_mask = land.astype(jnp.float32)
    weight = edge_weight * ocean_mask
    weight_sums = neighbour_sum(weight[None, :])[0]

    def to_columns(segment):
        full_cols = lax.all_to_all(segment, "depth", split_axis=2, concat_axis=1, tiled=True)
        return full_cols.reshape(FEATURES, full_cols.shape[2])

    def to_segments(values):
        shaped = values.reshape(2, LEVELS, values.shape[1])
        segment_part = lax.all_to_all(shaped, "depth", split_axis=1, concat_axis=2, tiled=True)
        return segment_part

    state_now = initial_state
    caches = []
    for step_index in range(TIME_STEPS):
        inputs = to_columns(state_now.astype(jnp.bfloat16))
        tendency, saved_cache = closure_forward(inputs, params)
        caches.append(saved_cache)
        change = diffuse(state_now, weight, weight_sums)
        state_now = (
            state_now
            + diffuse_coef * change
            + step_size * ocean_mask[None, None, :] * to_segments(tendency)
        )
    adjoint = ocean_mask[None, None, :] * (state_now - observed)
    grad_list = []
    for step_index in reversed(range(TIME_STEPS)):
        upstream = to_columns(
            (step_size * ocean_mask[None, None, :] * adjoint).astype(jnp.bfloat16)
        )
        back_grad, param_grads = closure_backward(upstream, caches[step_index], params)
        grad_list.append(param_grads)
        spread = diffuse(adjoint, weight, weight_sums)
        adjoint = adjoint + diffuse_coef * spread + to_segments(back_grad)
    totals = grad_list[0]
    for param_grads in grad_list[1:]:
        totals = tuple((total + gradient for total, gradient in zip(totals, param_grads)))
    summed = reduced_gradients(totals)
    grad_scale = 1.0 / (lax.axis_size("tile") * TILE_CELLS)
    return (
        state_now,
        adjoint,
        summed[0] * grad_scale,
        summed[1] * grad_scale,
        summed[2] * grad_scale,
        summed[3] * grad_scale,
        summed[4] * grad_scale,
        summed[5] * grad_scale,
    )


def solution(mesh):
    return jax.shard_map(
        body,
        mesh=mesh,
        in_specs=(
            P(None, "depth", "tile"),
            P(None, "depth", "tile"),
            P("tile"),
            P("tile"),
            P(),
            P(),
            P(),
            P(),
            P(),
            P(),
        ),
        out_specs=(
            P(None, "depth", "tile"),
            P(None, "depth", "tile"),
            P(),
            P(),
            P(),
            P(),
            P(),
            P(),
        ),
        check_vma=False,
    )
```

profile of v0, /device:TPU:0, one launch (start us, length us, event | category | flops | bytes accessed | tf_op | source)
XLA Modules:
  0.0 191.3 jit_solution(9956939731741169588)
XLA Ops:
  1.7 3.4 %collective-permute-start.4 = (f32[1,1,2,32]{3,2,1,0:T(2,128)S(1)}, f32[1,1,2,32]{3,2,1,0:T(2,128)S(1)}, u32[]{:S(2)}, u32[]{:S(2)}) collective-permute-start(f32[1,1,2,32]{3,2,1,0:T(2,128)S(1)} %maximum_bitcast_fusion.4), channel_id=1, source_target_pairs={{4,0},{8,4},{12,8},{16,12},{20,16},{24,20},{28,24},{0,28},{5,1},{9... | collective-permute-start | bytes 776 | tf_op jit(solution)/shard_map/ppermute | solution.py:24
  6.5 2.7 %collective-permute-start.1 = (f32[1,16,2,32]{3,1,2,0:T(8,128)S(1)}, f32[1,16,2,32]{3,1,2,0:T(8,128)S(1)}, u32[]{:S(2)}, u32[]{:S(2)}) collective-permute-start(f32[1,16,2,32]{3,1,2,0:T(8,128)S(1)} %maximum_bitcast_fusion), channel_id=1, source_target_pairs={{4,0},{8,4},{12,8},{16,12},{20,16},{24,20},{28,24},{0,28},{5,1},{9... | collective-permute-start | bytes 12296 | tf_op jit(solution)/shard_map/ppermute | solution.py:24
  12.1 4.9 %all-to-all-start = ((bf16[4,2,2048]{2,1,0:T(2,128)(2,1)}), bf16[4,2,2048]{2,1,0:T(2,128)(2,1)S(1)}, u32[]{:S(2)}, u32[]{:S(2)}) async-start(bf16[4,2,2048]{2,1,0:T(2,128)(2,1)} %reshape.430), calls=%async_computation | async-start | bytes 65536 | tf_op jit(solution)/shard_map/all_to_all | solution.py:185
  27.3 4.8 %all-to-all-start.1 = ((f32[2,32,256]{2,0,1:T(2,128)}), f32[2,32,256]{2,0,1:T(2,128)S(1)}, u32[]{:S(2)}, u32[]{:S(2)}) async-start(f32[2,32,256]{2,0,1:T(2,128)} %copy.161), calls=%async_computation.1 | async-start | bytes 131072 | tf_op jit(solution)/shard_map/all_to_all | solution.py:190
  32.5 5.4 %all-to-all-done.1 = f32[2,32,256]{2,0,1:T(2,128)S(1)} async-done(((f32[2,32,256]{2,0,1:T(2,128)}), f32[2,32,256]{2,0,1:T(2,128)S(1)}, u32[]{:S(2)}, u32[]{:S(2)}) %all-to-all-start.1) | async-done | bytes 65568 | tf_op jit(solution)/shard_map/all_to_all | solution.py:190
  43.0 3.3 %all-to-all-start.2 = ((bf16[4,2,2048]{2,1,0:T(2,128)(2,1)}), bf16[4,2,2048]{2,1,0:T(2,128)(2,1)S(1)}, u32[]{:S(2)}, u32[]{:S(2)}) async-start(bf16[4,2,2048]{2,1,0:T(2,128)(2,1)} %reshape.432), calls=%async_computation.2 | async-start | bytes 65536 | tf_op jit(solution)/shard_map/all_to_all | solution.py:185
  48.1 3.8 %all-to-all-done.2 = bf16[4,2,2048]{2,1,0:T(2,128)(2,1)S(1)} async-done(((bf16[4,2,2048]{2,1,0:T(2,128)(2,1)}), bf16[4,2,2048]{2,1,0:T(2,128)(2,1)S(1)}, u32[]{:S(2)}, u32[]{:S(2)}) %all-to-all-start.2) | async-done | bytes 32800 | tf_op jit(solution)/shard_map/all_to_all | solution.py:185
  56.4 3.9 %all-to-all-start.3 = ((f32[2,32,256]{2,0,1:T(2,128)}), f32[2,32,256]{2,0,1:T(2,128)}, u32[]{:S(2)}, u32[]{:S(2)}) async-start(f32[2,32,256]{2,0,1:T(2,128)} %copy.168), calls=%async_computation.3 | async-start | bytes 131072 | tf_op jit(solution)/shard_map/all_to_all | solution.py:190
  61.4 4.7 %all-to-all-done.3 = f32[2,32,256]{2,0,1:T(2,128)} async-done(((f32[2,32,256]{2,0,1:T(2,128)}), f32[2,32,256]{2,0,1:T(2,128)}, u32[]{:S(2)}, u32[]{:S(2)}) %all-to-all-start.3) | async-done | bytes 65568 | tf_op jit(solution)/shard_map/all_to_all | solution.py:190
  71.9 3.4 %all-to-all-start.4 = ((bf16[4,2,2048]{2,1,0:T(2,128)(2,1)}), bf16[4,2,2048]{2,1,0:T(2,128)(2,1)S(1)}, u32[]{:S(2)}, u32[]{:S(2)}) async-start(bf16[4,2,2048]{2,1,0:T(2,128)(2,1)} %reshape.434), calls=%async_computation.4 | async-start | bytes 65536 | tf_op jit(solution)/shard_map/all_to_all | solution.py:185
  76.3 4.6 %all-to-all-done.4 = bf16[4,2,2048]{2,1,0:T(2,128)(2,1)S(1)} async-done(((bf16[4,2,2048]{2,1,0:T(2,128)(2,1)}), bf16[4,2,2048]{2,1,0:T(2,128)(2,1)S(1)}, u32[]{:S(2)}, u32[]{:S(2)}) %all-to-all-start.4) | async-done | bytes 32800 | tf_op jit(solution)/shard_map/all_to_all | solution.py:185
  86.5 3.3 %all-to-all-start.5 = ((f32[2,32,256]{2,0,1:T(2,128)}), f32[2,32,256]{2,0,1:T(2,128)S(1)}, u32[]{:S(2)}, u32[]{:S(2)}) async-start(f32[2,32,256]{2,0,1:T(2,128)} %copy.175), calls=%async_computation.5 | async-start | bytes 131072 | tf_op jit(solution)/shard_map/all_to_all | solution.py:190
  90.0 5.5 %all-to-all-done.5 = f32[2,32,256]{2,0,1:T(2,128)S(1)} async-done(((f32[2,32,256]{2,0,1:T(2,128)}), f32[2,32,256]{2,0,1:T(2,128)S(1)}, u32[]{:S(2)}, u32[]{:S(2)}) %all-to-all-start.5) | async-done | bytes 65568 | tf_op jit(solution)/shard_map/all_to_all | solution.py:190
  97.7 3.3 %all-to-all-start.6 = ((bf16[4,2,2048]{2,1,0:T(2,128)(2,1)}), bf16[4,2,2048]{2,1,0:T(2,128)(2,1)S(1)}, u32[]{:S(2)}, u32[]{:S(2)}) async-start(bf16[4,2,2048]{2,1,0:T(2,128)(2,1)} %reshape.436), calls=%async_computation.6 | async-start | bytes 65536 | tf_op jit(solution)/shard_map/all_to_all | solution.py:185
  101.8 4.8 %all-to-all-done.6 = bf16[4,2,2048]{2,1,0:T(2,128)(2,1)S(1)} async-done(((bf16[4,2,2048]{2,1,0:T(2,128)(2,1)}), bf16[4,2,2048]{2,1,0:T(2,128)(2,1)S(1)}, u32[]{:S(2)}, u32[]{:S(2)}) %all-to-all-start.6) | async-done | bytes 32800 | tf_op jit(solution)/shard_map/all_to_all | solution.py:185
  119.7 2.5 %collective-permute-done.15 = f32[416,640]{1,0:T(8,128)} collective-permute-done((f32[416,640]{1,0:T(8,128)}, f32[416,640]{1,0:T(8,128)}, u32[]{:S(2)}, u32[]{:S(2)}) %collective-permute-start.15) | collective-permute-done | bytes 1064992 | tf_op jit(solution)/shard_map/ppermute | solution.py:116
  124.7 8.5 %collective-permute-done.16 = f32[208,640]{1,0:T(8,128)S(1)} collective-permute-done((f32[208,640]{1,0:T(8,128)S(1)}, f32[208,640]{1,0:T(8,128)S(1)}, u32[]{:S(2)}, u32[]{:S(2)}) %collective-permute-start.16) | collective-permute-done | bytes 532512 | tf_op jit(solution)/shard_map/ppermute | solution.py:116
  134.9 4.9 %collective-permute-done.17 = f32[104,640]{1,0:T(8,128)S(1)} collective-permute-done((f32[104,640]{1,0:T(8,128)S(1)}, f32[104,640]{1,0:T(8,128)S(1)}, u32[]{:S(2)}, u32[]{:S(2)}) %collective-permute-start.17) | collective-permute-done | bytes 266272 | tf_op jit(solution)/shard_map/ppermute | solution.py:116
  140.7 5.9 %collective-permute-done.18 = f32[104,640]{1,0:T(8,128)S(1)} collective-permute-done((f32[104,640]{1,0:T(8,128)S(1)}, f32[104,640]{1,0:T(8,128)S(1)}, u32[]{:S(2)}, u32[]{:S(2)}) %collective-permute-start.18) | collective-permute-done | bytes 266272 | tf_op jit(solution)/shard_map/ppermute | solution.py:116
  147.7 11.4 %collective-permute-done.19 = f32[104,640]{1,0:T(8,128)S(1)} collective-permute-done((f32[104,640]{1,0:T(8,128)S(1)}, f32[104,640]{1,0:T(8,128)S(1)}, u32[]{:S(2)}, u32[]{:S(2)}) %collective-permute-start.19) | collective-permute-done | bytes 266272 | tf_op jit(solution)/shard_map/ppermute | solution.py:116
  161.2 4.6 %collective-permute-done.20 = f32[104,640]{1,0:T(8,128)S(1)} collective-permute-done((f32[104,640]{1,0:T(8,128)S(1)}, f32[104,640]{1,0:T(8,128)S(1)}, u32[]{:S(2)}, u32[]{:S(2)}) %collective-permute-start.20) | collective-permute-done | bytes 266272 | tf_op jit(solution)/shard_map/ppermute | solution.py:116
  169.8 5.4 %collective-permute-done.21 = f32[208,640]{1,0:T(8,128)S(1)} collective-permute-done((f32[208,640]{1,0:T(8,128)S(1)}, f32[208,640]{1,0:T(8,128)S(1)}, u32[]{:S(2)}, u32[]{:S(2)}) %collective-permute-start.21) | collective-permute-done | bytes 532512 | tf_op jit(solution)/shard_map/ppermute | solution.py:116
  178.3 3.3 %all-to-all-start.7 = ((f32[2,32,256]{2,0,1:T(2,128)}), f32[2,32,256]{2,0,1:T(2,128)S(1)}, u32[]{:S(2)}, u32[]{:S(2)}) async-start(f32[2,32,256]{2,0,1:T(2,128)} %copy.182), calls=%async_computation.7 | async-start | bytes 131072 | tf_op jit(solution)/shard_map/all_to_all | solution.py:190
  183.3 4.0 %all-to-all-done.7 = f32[2,32,256]{2,0,1:T(2,128)S(1)} async-done(((f32[2,32,256]{2,0,1:T(2,128)}), f32[2,32,256]{2,0,1:T(2,128)S(1)}, u32[]{:S(2)}, u32[]{:S(2)}) %all-to-all-start.7) | async-done | bytes 65568 | tf_op jit(solution)/shard_map/all_to_all | solution.py:190
  (260 shorter events, 77.5 us)
Async XLA Ops:
  1.7 18.1 %collective-permute-start.4 = (f32[1,1,2,32]{3,2,1,0:T(2,128)S(1)}, f32[1,1,2,32]{3,2,1,0:T(2,128)S(1)}, u32[]{:S(2)}, u32[]{:S(2)}) collective-permute-start(f32[1,1,2,32]{3,2,1,0:T(2,128)S(1)} %maximum_bitcast_fusion.4), channel_id=1, source_target_pairs={{4,0},{8,4},{12,8},{16,12},{20,16},{24,20},{28,24},{0,28},{5,1},{9... | collective-permute-start | bytes 776 | tf_op jit(solution)/shard_map/ppermute | solution.py:24
  5.1 12.8 %collective-permute-start.3 = (f32[1,1,2,32]{3,2,1,0:T(2,128)S(1)}, f32[1,1,2,32]{3,2,1,0:T(2,128)S(1)}, u32[]{:S(2)}, u32[]{:S(2)}) collective-permute-start(f32[1,1,2,32]{3,2,1,0:T(2,128)S(1)} %maximum_bitcast_fusion.4), channel_id=1, source_target_pairs={{0,4},{4,8},{8,12},{12,16},{16,20},{20,24},{24,28},{28,0},{1,5},{5... | collective-permute-start | bytes 776 | tf_op jit(solution)/shard_map/ppermute | solution.py:22
  6.5 15.3 %collective-permute-start.1 = (f32[1,16,2,32]{3,1,2,0:T(8,128)S(1)}, f32[1,16,2,32]{3,1,2,0:T(8,128)S(1)}, u32[]{:S(2)}, u32[]{:S(2)}) collective-permute-start(f32[1,16,2,32]{3,1,2,0:T(8,128)S(1)} %maximum_bitcast_fusion), channel_id=1, source_target_pairs={{4,0},{8,4},{12,8},{16,12},{20,16},{24,20},{28,24},{0,28},{5,1},{9... | collective-permute-start | bytes 12296 | tf_op jit(solution)/shard_map/ppermute | solution.py:24
  9.2 12.6 %collective-permute-start = (f32[1,16,2,32]{3,1,2,0:T(8,128)S(1)}, f32[1,16,2,32]{3,1,2,0:T(8,128)S(1)}, u32[]{:S(2)}, u32[]{:S(2)}) collective-permute-start(f32[1,16,2,32]{3,1,2,0:T(8,128)S(1)} %maximum_bitcast_fusion), channel_id=1, source_target_pairs={{0,4},{4,8},{8,12},{12,16},{16,20},{20,24},{24,28},{28,0},{1,5},{5... | collective-permute-start | bytes 12296 | tf_op jit(solution)/shard_map/ppermute | solution.py:22
  9.2 10.3 %collective-permute-start.5 = (f32[1,2,32]{2,1,0:T(2,128)S(1)}, f32[1,2,32]{2,1,0:T(2,128)S(1)}, u32[]{:S(2)}, u32[]{:S(2)}) collective-permute-start(f32[1,2,32]{2,1,0:T(2,128)S(1)} %pad_maximum_fusion.4), channel_id=1, source_target_pairs={{0,16},{4,20},{8,24},{12,28},{16,0},{20,4},{24,8},{28,12},{1,17},{... | collective-permute-start | bytes 776 | tf_op jit(solution)/shard_map/ppermute | solution.py:33
  12.1 10.5 %all-to-all-start = ((bf16[4,2,2048]{2,1,0:T(2,128)(2,1)}), bf16[4,2,2048]{2,1,0:T(2,128)(2,1)S(1)}, u32[]{:S(2)}, u32[]{:S(2)}) async-start(bf16[4,2,2048]{2,1,0:T(2,128)(2,1)} %reshape.430), calls=%async_computation | async-start | bytes 65536 | tf_op jit(solution)/shard_map/all_to_all | solution.py:185
  27.3 10.6 %all-to-all-start.1 = ((f32[2,32,256]{2,0,1:T(2,128)}), f32[2,32,256]{2,0,1:T(2,128)S(1)}, u32[]{:S(2)}, u32[]{:S(2)}) async-start(f32[2,32,256]{2,0,1:T(2,128)} %copy.161), calls=%async_computation.1 | async-start | bytes 131072 | tf_op jit(solution)/shard_map/all_to_all | solution.py:190
  38.4 7.8 %collective-permute-start.7 = (f32[1,16,2,32]{3,1,2,0:T(8,128)S(1)}, f32[1,16,2,32]{3,1,2,0:T(8,128)S(1)}, u32[]{:S(2)}, u32[]{:S(2)}) collective-permute-start(f32[1,16,2,32]{3,1,2,0:T(8,128)S(1)} %maximum_bitcast_fusion.1), channel_id=1, source_target_pairs={{4,0},{8,4},{12,8},{16,12},{20,16},{24,20},{28,24},{0,28},{5,1},{9... | collective-permute-start | bytes 12296 | tf_op jit(solution)/shard_map/ppermute | solution.py:24
  38.5 7.8 %collective-permute-start.6 = (f32[1,16,2,32]{3,1,2,0:T(8,128)S(1)}, f32[1,16,2,32]{3,1,2,0:T(8,128)S(1)}, u32[]{:S(2)}, u32[]{:S(2)}) collective-permute-start(f32[1,16,2,32]{3,1,2,0:T(8,128)S(1)} %maximum_bitcast_fusion.1), channel_id=1, source_target_pairs={{0,4},{4,8},{8,12},{12,16},{16,20},{20,24},{24,28},{28,0},{1,5},{5... | collective-permute-start | bytes 12296 | tf_op jit(solution)/shard_map/ppermute | solution.py:22
  39.2 7.1 %collective-permute-start.8 = (f32[16,2,32]{2,1,0:T(2,128)S(1)}, f32[16,2,32]{2,1,0:T(2,128)S(1)}, u32[]{:S(2)}, u32[]{:S(2)}) collective-permute-start(f32[16,2,32]{2,1,0:T(2,128)S(1)} %pad_maximum_fusion.1), channel_id=1, source_target_pairs={{0,16},{4,20},{8,24},{12,28},{16,0},{20,4},{24,8},{28,12},{1,17},{... | collective-permute-start | bytes 12296 | tf_op jit(solution)/shard_map/ppermute | solution.py:33
  43.0 8.9 %all-to-all-start.2 = ((bf16[4,2,2048]{2,1,0:T(2,128)(2,1)}), bf16[4,2,2048]{2,1,0:T(2,128)(2,1)S(1)}, u32[]{:S(2)}, u32[]{:S(2)}) async-start(bf16[4,2,2048]{2,1,0:T(2,128)(2,1)} %reshape.432), calls=%async_computation.2 | async-start | bytes 65536 | tf_op jit(solution)/shard_map/all_to_all | solution.py:185
  56.4 9.7 %all-to-all-start.3 = ((f32[2,32,256]{2,0,1:T(2,128)}), f32[2,32,256]{2,0,1:T(2,128)}, u32[]{:S(2)}, u32[]{:S(2)}) async-start(f32[2,32,256]{2,0,1:T(2,128)} %copy.168), calls=%async_computation.3 | async-start | bytes 131072 | tf_op jit(solution)/shard_map/all_to_all | solution.py:190
  71.9 9.0 %all-to-all-start.4 = ((bf16[4,2,2048]{2,1,0:T(2,128)(2,1)}), bf16[4,2,2048]{2,1,0:T(2,128)(2,1)S(1)}, u32[]{:S(2)}, u32[]{:S(2)}) async-start(bf16[4,2,2048]{2,1,0:T(2,128)(2,1)} %reshape.434), calls=%async_computation.4 | async-start | bytes 65536 | tf_op jit(solution)/shard_map/all_to_all | solution.py:185
  86.5 9.0 %all-to-all-start.5 = ((f32[2,32,256]{2,0,1:T(2,128)}), f32[2,32,256]{2,0,1:T(2,128)S(1)}, u32[]{:S(2)}, u32[]{:S(2)}) async-start(f32[2,32,256]{2,0,1:T(2,128)} %copy.175), calls=%async_computation.5 | async-start | bytes 131072 | tf_op jit(solution)/shard_map/all_to_all | solution.py:190
  97.7 8.9 %all-to-all-start.6 = ((bf16[4,2,2048]{2,1,0:T(2,128)(2,1)}), bf16[4,2,2048]{2,1,0:T(2,128)(2,1)S(1)}, u32[]{:S(2)}, u32[]{:S(2)}) async-start(bf16[4,2,2048]{2,1,0:T(2,128)(2,1)} %reshape.436), calls=%async_computation.6 | async-start | bytes 65536 | tf_op jit(solution)/shard_map/all_to_all | solution.py:185
  123.8 9.3 %collective-permute-start.16 = (f32[208,640]{1,0:T(8,128)S(1)}, f32[208,640]{1,0:T(8,128)S(1)}, u32[]{:S(2)}, u32[]{:S(2)}) collective-permute-start(f32[208,640]{1,0:T(8,128)S(1)} %dynamic-slice_bitcast_fusion.1), channel_id=1, source_target_pairs={{0,8},{4,20},{8,0},{12,28},{16,24},{20,4},{24,16},{28,12},{1,9},{5... | collective-permute-start | bytes 1597448 | tf_op jit(solution)/shard_map/ppermute | solution.py:116
  139.8 6.8 %collective-permute-start.18 = (f32[104,640]{1,0:T(8,128)S(1)}, f32[104,640]{1,0:T(8,128)S(1)}, u32[]{:S(2)}, u32[]{:S(2)}) collective-permute-start(f32[104,640]{1,0:T(8,128)S(1)} %bitcast_add_fusion.2), channel_id=1, source_target_pairs={{0,1},{1,0},{2,3},{3,2},{4,5},{5,4},{6,7},{7,6},{8,9},{9,8},{10,11... | collective-permute-start | bytes 798728 | tf_op jit(solution)/shard_map/ppermute | solution.py:116
  146.6 12.5 %collective-permute-start.19 = (f32[104,640]{1,0:T(8,128)S(1)}, f32[104,640]{1,0:T(8,128)S(1)}, u32[]{:S(2)}, u32[]{:S(2)}) collective-permute-start(f32[104,640]{1,0:T(8,128)S(1)} %add.383), channel_id=1, source_target_pairs={{0,2},{1,3},{2,0},{3,1},{4,6},{5,7},{6,4},{7,5},{8,10},{9,11},{10,... | collective-permute-start | bytes 798728 | tf_op jit(solution)/shard_map/ppermute | solution.py:116
  160.7 15.8 %collective-permute-start.13 = (f32[1,16,2,32]{3,1,2,0:T(8,128)S(1)}, f32[1,16,2,32]{3,1,2,0:T(8,128)S(1)}, u32[]{:S(2)}, u32[]{:S(2)}) collective-permute-start(f32[1,16,2,32]{3,1,2,0:T(8,128)S(1)} %maximum_bitcast_fusion.3), channel_id=1, source_target_pairs={{4,0},{8,4},{12,8},{16,12},{20,16},{24,20},{28,24},{0,28},{5,1},{9... | collective-permute-start | bytes 12296 | tf_op jit(solution)/shard_map/ppermute | solution.py:24
  160.9 14.4 %collective-permute-start.12 = (f32[1,16,2,32]{3,1,2,0:T(8,128)S(1)}, f32[1,16,2,32]{3,1,2,0:T(8,128)S(1)}, u32[]{:S(2)}, u32[]{:S(2)}) collective-permute-start(f32[1,16,2,32]{3,1,2,0:T(8,128)S(1)} %maximum_bitcast_fusion.3), channel_id=1, source_target_pairs={{0,4},{4,8},{8,12},{12,16},{16,20},{20,24},{24,28},{28,0},{1,5},{5... | collective-permute-start | bytes 12296 | tf_op jit(solution)/shard_map/ppermute | solution.py:22
  165.8 9.3 %collective-permute-start.21 = (f32[208,640]{1,0:T(8,128)S(1)}, f32[208,640]{1,0:T(8,128)S(1)}, u32[]{:S(2)}, u32[]{:S(2)}) collective-permute-start(f32[208,640]{1,0:T(8,128)S(1)} %bitcast.194), channel_id=1, source_target_pairs={{0,8},{4,20},{8,0},{12,28},{16,24},{20,4},{24,16},{28,12},{1,9},{5... | collective-permute-start | bytes 1597448 | tf_op jit(solution)/shard_map/ppermute | solution.py:116
  166.7 8.6 %collective-permute-start.14 = (f32[16,2,32]{2,1,0:T(2,128)S(1)}, f32[16,2,32]{2,1,0:T(2,128)S(1)}, u32[]{:S(2)}, u32[]{:S(2)}) collective-permute-start(f32[16,2,32]{2,1,0:T(2,128)S(1)} %pad_maximum_fusion.3), channel_id=1, source_target_pairs={{0,16},{4,20},{8,24},{12,28},{16,0},{20,4},{24,8},{28,12},{1,17},{... | collective-permute-start | bytes 12296 | tf_op jit(solution)/shard_map/ppermute | solution.py:33
  175.3 12.8 %collective-permute-start.22 = (f32[416,640]{1,0:T(8,128)S(1)}, f32[416,640]{1,0:T(8,128)S(1)}, u32[]{:S(2)}, u32[]{:S(2)}) collective-permute-start(f32[416,640]{1,0:T(8,128)S(1)} %bitcast.190), channel_id=1, source_target_pairs={{0,4},{4,0},{8,12},{12,8},{16,20},{20,16},{24,28},{28,24},{1,5},{5... | collective-permute-start | bytes 3194888 | tf_op jit(solution)/shard_map/ppermute | solution.py:116
  178.3 9.0 %all-to-all-start.7 = ((f32[2,32,256]{2,0,1:T(2,128)}), f32[2,32,256]{2,0,1:T(2,128)S(1)}, u32[]{:S(2)}, u32[]{:S(2)}) async-start(f32[2,32,256]{2,0,1:T(2,128)} %copy.182), calls=%async_computation.7 | async-start | bytes 131072 | tf_op jit(solution)/shard_map/all_to_all | solution.py:190
  (35 other events, 234.9 us)
where the time goes:
time: 193 us; the launch traced here: 191 us
  waiting for transfers between devices  77.9 us (40%)
  starting transfers between devices  49.9 us (26%)
  local copies, waits for them, and re-layouts  32.4 us (17%)
  matrix products  15.8 us (8%)
  other arithmetic  13.6 us (7%)
    ppermute x8, waiting for transfers between devices, swapped(): lax.ppermute(x, axis, [(i, i ^ (odd_bit if i & 1 else even_bit)) for i in...  43.1 us
    all_to_all x4, waiting for transfers between devices, to_segments(): lax.all_to_all(shaped, 'depth', split_axis=1, concat_axis=2, tiled=True)  19.7 us
    all_to_all x4, starting transfers between devices, to_segments(): lax.all_to_all(shaped, 'depth', split_axis=1, concat_axis=2, tiled=True)  15.3 us
    all_to_all x4, starting transfers between devices, to_columns(): lax.all_to_all(segment, 'depth', split_axis=2, concat_axis=1, tiled=True)  14.8 us
    all_to_all x4, waiting for transfers between devices, to_columns(): lax.all_to_all(segment, 'depth', split_axis=2, concat_axis=1, tiled=True)  13.4 us
    unnamed x65, local copies, waits for them, and re-layouts  9.16 us
    ppermute x8, starting transfers between devices, swapped(): lax.ppermute(x, axis, [(i, i ^ (odd_bit if i & 1 else even_bit)) for i in...  6.47 us
    ppermute x5, starting transfers between devices, with_halo(): lax.ppermute(head, axis, [((i + 1) % count, i) for i in range(count)])  6.4 us
  transfers between devices with their start and end apart: 31, of which 16 were waited for; matrix products, arithmetic and copies ran while one was open for 12% of the time, Pallas kernels for 0%

commit v1 on v0

--- a/solution.py
+++ b/solution.py
@@ -10,6 +10,22 @@
 TILE_CELLS = 1024
 diffuse_coef = 0.2
 step_size = 0.5
+
+
+def pairwise_exchange(x, axis, split, join):
+    ways, here = (lax.axis_size(axis), lax.axis_index(axis))
+    width = x.shape[split] // ways
+    shape = list(x.shape)
+    shape[split] = width
+    height = shape[join]
+    shape[join] = height * ways
+    full = jnp.zeros(shape, x.dtype)
+    for mask in range(ways):
+        part = lax.dynamic_slice_in_dim(x, (here ^ mask) * width, width, axis=split)
+        if mask:
+            part = lax.ppermute(part, axis, [(d, d ^ mask) for d in range(ways)])
+        full = lax.dynamic_update_slice_in_dim(full, part, (here ^ mask) * height, axis=join)
+    return full
 
 
 def with_halo(cells, sides, width):
@@ -187,7 +203,7 @@
 
     def to_segments(values):
         shaped = values.reshape(2, LEVELS, values.shape[1])
-        segment_part = lax.all_to_all(shaped, "depth", split_axis=1, concat_axis=2, tiled=True)
+        segment_part = pairwise_exchange(shaped, "depth", 1, 2)
         return segment_part
 
     state_now = initial_state

time: 193 us -> 185 us (0.959)
  waiting for transfers between devices: 77.9 us -> 68.9 us
  starting transfers between devices: 49.9 us -> 52.4 us
    all_to_all x4 -> x0, waiting for transfers between devices: 19.7 us -> none  [to_segments(): lax.all_to_all(shaped, 'depth', split_axis=1, concat_axis=2, tiled=True)]
    all_to_all x4 -> x0, starting transfers between devices: 15.3 us -> none  [to_segments(): lax.all_to_all(shaped, 'depth', split_axis=1, concat_axis=2, tiled=True)]
    ppermute x0 -> x12, starting transfers between devices: none -> 15.1 us  [pairwise_exchange(): part = lax.ppermute(part, axis, [(d, d ^ mask) for d in range(ways)])]
    ppermute x0 -> x12, waiting for transfers between devices: none -> 12.4 us  [pairwise_exchange(): part = lax.ppermute(part, axis, [(d, d ^ mask) for d in range(ways)])]
    ppermute x8, waiting for transfers between devices: 43.1 us -> 38.8 us  [swapped(): lax.ppermute(x, axis, [(i, i ^ (odd_bit if i & 1 else even_bit)) for i in...]
    reshape x4 -> x0, local copies, waits for them, and re-layouts: 2.76 us -> none  [to_segments(): shaped = values.reshape(2, LEVELS, values.shape[1])]
    dynamic_update_slice x0 -> x12, local copies, waits for them, and re-layouts: none -> 2.56 us  [pairwise_exchange(): lax.dynamic_update_slice_in_dim(full, part, (here ^ mask) * height, axis=...]
    ppermute x5, waiting for transfers between devices: 1.68 us -> 4.18 us  [passed_along(): lax.ppermute(x, axis, [(i, (i + by) % length) for i in range(length)])]
  transfers between devices with their start and end apart: 31 -> 39, of which waited for: 16 -> 19; matrix products, arithmetic and copies ran while one was open for 12% -> 13% of each run, Pallas kernels for 0% -> 0%
where the time goes in v1:
time: 185 us; the launch traced here: 184 us
  waiting for transfers between devices  68.9 us (37%)
  starting transfers between devices  52.4 us (28%)
  local copies, waits for them, and re-layouts  32 us (17%)
  matrix products  15.9 us (9%)
  other arithmetic  13 us (7%)
    ppermute x8, waiting for transfers between devices, swapped(): lax.ppermute(x, axis, [(i, i ^ (odd_bit if i & 1 else even_bit)) for i in...  38.8 us
    all_to_all x4, starting transfers between devices, to_columns(): lax.all_to_all(segment, 'depth', split_axis=2, concat_axis=1, tiled=True)  15.7 us
    ppermute x12, starting transfers between devices, pairwise_exchange(): part = lax.ppermute(part, axis, [(d, d ^ mask) for d in range(ways)])  15.1 us
    all_to_all x4, waiting for transfers between devices, to_columns(): lax.all_to_all(segment, 'depth', split_axis=2, concat_axis=1, tiled=True)  13.5 us
    ppermute x12, waiting for transfers between devices, pairwise_exchange(): part = lax.ppermute(part, axis, [(d, d ^ mask) for d in range(ways)])  12.4 us
    unnamed x71, local copies, waits for them, and re-layouts  9.15 us
    ppermute x5, starting transfers between devices, with_halo(): lax.ppermute(head, axis, [((i + 1) % count, i) for i in range(count)])  8.88 us
    ppermute x8, starting transfers between devices, swapped(): lax.ppermute(x, axis, [(i, i ^ (odd_bit if i & 1 else even_bit)) for i in...  5.86 us
  transfers between devices with their start and end apart: 39, of which 19 were waited for; matrix products, arithmetic and copies ran while one was open for 13% of the time, Pallas kernels for 0%

profile of v1, /device:TPU:0, one launch (start us, length us, event | category | flops | bytes accessed | tf_op | source)
XLA Modules:
  0.0 184.0 jit_solution(15736894074795507236)
XLA Ops:
  1.7 3.4 %collective-permute-start.4 = (f32[1,1,2,32]{3,2,1,0:T(2,128)S(1)}, f32[1,1,2,32]{3,2,1,0:T(2,128)S(1)}, u32[]{:S(2)}, u32[]{:S(2)}) collective-permute-start(f32[1,1,2,32]{3,2,1,0:T(2,128)S(1)} %maximum_bitcast_fusion.4), channel_id=1, source_target_pairs={{4,0},{8,4},{12,8},{16,12},{20,16},{24,20},{28,24},{0,28},{5,1},{9... | collective-permute-start | bytes 776 | tf_op jit(solution)/shard_map/ppermute | solution.py:40
  6.5 2.7 %collective-permute-start.1 = (f32[1,16,2,32]{3,1,2,0:T(8,128)S(1)}, f32[1,16,2,32]{3,1,2,0:T(8,128)S(1)}, u32[]{:S(2)}, u32[]{:S(2)}) collective-permute-start(f32[1,16,2,32]{3,1,2,0:T(8,128)S(1)} %maximum_bitcast_fusion), channel_id=1, source_target_pairs={{4,0},{8,4},{12,8},{16,12},{20,16},{24,20},{28,24},{0,28},{5,1},{9... | collective-permute-start | bytes 12296 | tf_op jit(solution)/shard_map/ppermute | solution.py:40
  12.1 4.9 %all-to-all-start = ((bf16[4,2,2048]{2,1,0:T(2,128)(2,1)}), bf16[4,2,2048]{2,1,0:T(2,128)(2,1)S(1)}, u32[]{:S(2)}, u32[]{:S(2)}) async-start(bf16[4,2,2048]{2,1,0:T(2,128)(2,1)} %reshape.430), calls=%async_computation | async-start | bytes 65536 | tf_op jit(solution)/shard_map/all_to_all | solution.py:201
  24.3 2.1 %multiply_convert_fusion.2 = (bf16[640,256]{0,1:T(8,128)(2,1)S(1)}, f32[640,256]{0,1:T(8,128)}) fusion(f32[640]{0:T(1024)} %param.23, bf16[640,640]{1,0:T(8,128)(2,1)S(1)} %copy-done, f32[640,256]{0,1:T(8,128)S(1)} %convolution_add_fusion.3), kind=kOutput, calls=%fused_computation.40 | convolution fusion | flops 211517440 | bytes 2460160 | tf_op jit(solution)/shard_map/dot_general | solution.py:89
  28.9 2.4 %collective-permute-start.8 = (f32[2,8,256]{2,1,0:T(8,128)S(1)}, f32[2,8,256]{2,1,0:T(8,128)S(1)}, u32[]{:S(2)}, u32[]{:S(2)}) collective-permute-start(f32[2,8,256]{2,1,0:T(8,128)S(1)} %get-tuple-element.101), channel_id=1, source_target_pairs={{0,3},{1,2},{2,1},{3,0},{4,7},{5,6},{6,5},{7,4},{8,11},{9,10},{10,... | collective-permute-start | bytes 49160 | tf_op jit(solution)/shard_map/ppermute | solution.py:26
  31.4 4.7 %collective-permute-done.7 = f32[2,8,256]{2,1,0:T(8,128)S(1)} collective-permute-done((f32[2,8,256]{2,1,0:T(8,128)S(1)}, f32[2,8,256]{2,1,0:T(8,128)S(1)}, u32[]{:S(2)}, u32[]{:S(2)}) %collective-permute-start.7) | collective-permute-done | bytes 16416 | tf_op jit(solution)/shard_map/ppermute | solution.py:26
  41.2 3.3 %all-to-all-start.1 = ((bf16[4,2,2048]{2,1,0:T(2,128)(2,1)}), bf16[4,2,2048]{2,1,0:T(2,128)(2,1)S(1)}, u32[]{:S(2)}, u32[]{:S(2)}) async-start(bf16[4,2,2048]{2,1,0:T(2,128)(2,1)} %reshape.432), calls=%async_computation.1 | async-start | bytes 65536 | tf_op jit(solution)/shard_map/all_to_all | solution.py:201
  46.4 3.8 %all-to-all-done.1 = bf16[4,2,2048]{2,1,0:T(2,128)(2,1)S(1)} async-done(((bf16[4,2,2048]{2,1,0:T(2,128)(2,1)}), bf16[4,2,2048]{2,1,0:T(2,128)(2,1)S(1)}, u32[]{:S(2)}, u32[]{:S(2)}) %all-to-all-start.1) | async-done | bytes 32800 | tf_op jit(solution)/shard_map/all_to_all | solution.py:201
  51.5 2.3 %multiply_convert_fusion = (bf16[640,256]{0,1:T(8,128)(2,1)S(1)}, f32[640,256]{0,1:T(8,128)}) fusion(f32[640]{0:T(1024)} %param.23, bf16[640,640]{1,0:T(8,128)(2,1)S(1)} %copy-done, f32[640,256]{0,1:T(8,128)S(1)} %fusion.3), kind=kOutput, calls=%fused_computation.36 | convolution fusion | flops 211517440 | bytes 2460160 | tf_op jit(solution)/shard_map/dot_general | solution.py:89
  68.2 3.9 %all-to-all-start.2 = ((bf16[4,2,2048]{2,1,0:T(2,128)(2,1)}), bf16[4,2,2048]{2,1,0:T(2,128)(2,1)S(1)}, u32[]{:S(2)}, u32[]{:S(2)}) async-start(bf16[4,2,2048]{2,1,0:T(2,128)(2,1)} %reshape.434), calls=%async_computation.2 | async-start | bytes 65536 | tf_op jit(solution)/shard_map/all_to_all | solution.py:201
  73.1 4.7 %all-to-all-done.2 = bf16[4,2,2048]{2,1,0:T(2,128)(2,1)S(1)} async-done(((bf16[4,2,2048]{2,1,0:T(2,128)(2,1)}), bf16[4,2,2048]{2,1,0:T(2,128)(2,1)S(1)}, u32[]{:S(2)}, u32[]{:S(2)}) %all-to-all-start.2) | async-done | bytes 32800 | tf_op jit(solution)/shard_map/all_to_all | solution.py:201
  86.6 3.2 %collective-permute-done.19 = f32[2,8,256]{2,1,0:T(8,128)S(1)} collective-permute-done((f32[2,8,256]{2,1,0:T(8,128)S(1)}, f32[2,8,256]{2,1,0:T(8,128)S(1)}, u32[]{:S(2)}, u32[]{:S(2)}) %collective-permute-start.19) | collective-permute-done | bytes 16416 | tf_op jit(solution)/shard_map/ppermute | solution.py:26
  92.0 3.7 %all-to-all-start.3 = ((bf16[4,2,2048]{2,1,0:T(2,128)(2,1)}), bf16[4,2,2048]{2,1,0:T(2,128)(2,1)S(1)}, u32[]{:S(2)}, u32[]{:S(2)}) async-start(bf16[4,2,2048]{2,1,0:T(2,128)(2,1)} %reshape.436), calls=%async_computation.3 | async-start | bytes 65536 | tf_op jit(solution)/shard_map/all_to_all | solution.py:201
  96.6 4.8 %all-to-all-done.3 = bf16[4,2,2048]{2,1,0:T(2,128)(2,1)S(1)} async-done(((bf16[4,2,2048]{2,1,0:T(2,128)(2,1)}), bf16[4,2,2048]{2,1,0:T(2,128)(2,1)S(1)}, u32[]{:S(2)}, u32[]{:S(2)}) %all-to-all-start.3) | async-done | bytes 32800 | tf_op jit(solution)/shard_map/all_to_all | solution.py:201
  114.4 2.5 %collective-permute-done.27 = f32[416,640]{1,0:T(8,128)} collective-permute-done((f32[416,640]{1,0:T(8,128)}, f32[416,640]{1,0:T(8,128)}, u32[]{:S(2)}, u32[]{:S(2)}) %collective-permute-start.27) | collective-permute-done | bytes 1064992 | tf_op jit(solution)/shard_map/ppermute | solution.py:132
  119.3 8.7 %collective-permute-done.28 = f32[208,640]{1,0:T(8,128)S(1)} collective-permute-done((f32[208,640]{1,0:T(8,128)S(1)}, f32[208,640]{1,0:T(8,128)S(1)}, u32[]{:S(2)}, u32[]{:S(2)}) %collective-permute-start.28) | collective-permute-done | bytes 532512 | tf_op jit(solution)/shard_map/ppermute | solution.py:132
  129.8 4.8 %collective-permute-done.29 = f32[104,640]{1,0:T(8,128)S(1)} collective-permute-done((f32[104,640]{1,0:T(8,128)S(1)}, f32[104,640]{1,0:T(8,128)S(1)}, u32[]{:S(2)}, u32[]{:S(2)}) %collective-permute-start.29) | collective-permute-done | bytes 266272 | tf_op jit(solution)/shard_map/ppermute | solution.py:132
  135.4 6.0 %collective-permute-done.30 = f32[104,640]{1,0:T(8,128)S(1)} collective-permute-done((f32[104,640]{1,0:T(8,128)S(1)}, f32[104,640]{1,0:T(8,128)S(1)}, u32[]{:S(2)}, u32[]{:S(2)}) %collective-permute-start.30) | collective-permute-done | bytes 266272 | tf_op jit(solution)/shard_map/ppermute | solution.py:132
  143.3 10.6 %collective-permute-done.31 = f32[104,640]{1,0:T(8,128)S(1)} collective-permute-done((f32[104,640]{1,0:T(8,128)S(1)}, f32[104,640]{1,0:T(8,128)S(1)}, u32[]{:S(2)}, u32[]{:S(2)}) %collective-permute-start.31) | collective-permute-done | bytes 266272 | tf_op jit(solution)/shard_map/ppermute | solution.py:132
  155.5 2.6 %collective-permute-start.22 = (f32[1,16,2,32]{3,1,2,0:T(8,128)S(1)}, f32[1,16,2,32]{3,1,2,0:T(8,128)S(1)}, u32[]{:S(2)}, u32[]{:S(2)}) collective-permute-start(f32[1,16,2,32]{3,1,2,0:T(8,128)S(1)} %maximum_bitcast_fusion.3), channel_id=1, source_target_pairs={{4,0},{8,4},{12,8},{16,12},{20,16},{24,20},{28,24},{0,28},{5,1},{9... | collective-permute-start | bytes 12296 | tf_op jit(solution)/shard_map/ppermute | solution.py:40
  162.7 2.5 %collective-permute-done.23 = f32[16,2,32]{2,1,0:T(2,128)S(1)} collective-permute-done((f32[16,2,32]{2,1,0:T(2,128)S(1)}, f32[16,2,32]{2,1,0:T(2,128)S(1)}, u32[]{:S(2)}, u32[]{:S(2)}) %collective-permute-start.23) | collective-permute-done | bytes 4128 | tf_op jit(solution)/shard_map/ppermute | solution.py:49
  165.2 4.8 %collective-permute-done.33 = f32[208,640]{1,0:T(8,128)S(1)} collective-permute-done((f32[208,640]{1,0:T(8,128)S(1)}, f32[208,640]{1,0:T(8,128)S(1)}, u32[]{:S(2)}, u32[]{:S(2)}) %collective-permute-start.33) | collective-permute-done | bytes 532512 | tf_op jit(solution)/shard_map/ppermute | solution.py:132
  175.3 2.5 %collective-permute-start.25 = (f32[2,8,256]{2,1,0:T(8,128)S(1)}, f32[2,8,256]{2,1,0:T(8,128)S(1)}, u32[]{:S(2)}, u32[]{:S(2)}) collective-permute-start(f32[2,8,256]{2,1,0:T(8,128)S(1)} %get-tuple-element.90), channel_id=1, source_target_pairs={{0,2},{1,3},{2,0},{3,1},{4,6},{5,7},{6,4},{7,5},{8,10},{9,11},{10,... | collective-permute-start | bytes 49160 | tf_op jit(solution)/shard_map/ppermute | solution.py:26
  177.8 2.3 %collective-permute-done.25 = f32[2,8,256]{2,1,0:T(8,128)S(1)} collective-permute-done((f32[2,8,256]{2,1,0:T(8,128)S(1)}, f32[2,8,256]{2,1,0:T(8,128)S(1)}, u32[]{:S(2)}, u32[]{:S(2)}) %collective-permute-start.25) | collective-permute-done | bytes 16416 | tf_op jit(solution)/shard_map/ppermute | solution.py:26
  (294 shorter events, 85.4 us)
Async XLA Ops:
  1.7 18.1 %collective-permute-start.4 = (f32[1,1,2,32]{3,2,1,0:T(2,128)S(1)}, f32[1,1,2,32]{3,2,1,0:T(2,128)S(1)}, u32[]{:S(2)}, u32[]{:S(2)}) collective-permute-start(f32[1,1,2,32]{3,2,1,0:T(2,128)S(1)} %maximum_bitcast_fusion.4), channel_id=1, source_target_pairs={{4,0},{8,4},{12,8},{16,12},{20,16},{24,20},{28,24},{0,28},{5,1},{9... | collective-permute-start | bytes 776 | tf_op jit(solution)/shard_map/ppermute | solution.py:40
  5.1 12.9 %collective-permute-start.3 = (f32[1,1,2,32]{3,2,1,0:T(2,128)S(1)}, f32[1,1,2,32]{3,2,1,0:T(2,128)S(1)}, u32[]{:S(2)}, u32[]{:S(2)}) collective-permute-start(f32[1,1,2,32]{3,2,1,0:T(2,128)S(1)} %maximum_bitcast_fusion.4), channel_id=1, source_target_pairs={{0,4},{4,8},{8,12},{12,16},{16,20},{20,24},{24,28},{28,0},{1,5},{5... | collective-permute-start | bytes 776 | tf_op jit(solution)/shard_map/ppermute | solution.py:38
  6.5 15.3 %collective-permute-start.1 = (f32[1,16,2,32]{3,1,2,0:T(8,128)S(1)}, f32[1,16,2,32]{3,1,2,0:T(8,128)S(1)}, u32[]{:S(2)}, u32[]{:S(2)}) collective-permute-start(f32[1,16,2,32]{3,1,2,0:T(8,128)S(1)} %maximum_bitcast_fusion), channel_id=1, source_target_pairs={{4,0},{8,4},{12,8},{16,12},{20,16},{24,20},{28,24},{0,28},{5,1},{9... | collective-permute-start | bytes 12296 | tf_op jit(solution)/shard_map/ppermute | solution.py:40
  9.2 12.6 %collective-permute-start = (f32[1,16,2,32]{3,1,2,0:T(8,128)S(1)}, f32[1,16,2,32]{3,1,2,0:T(8,128)S(1)}, u32[]{:S(2)}, u32[]{:S(2)}) collective-permute-start(f32[1,16,2,32]{3,1,2,0:T(8,128)S(1)} %maximum_bitcast_fusion), channel_id=1, source_target_pairs={{0,4},{4,8},{8,12},{12,16},{16,20},{20,24},{24,28},{28,0},{1,5},{5... | collective-permute-start | bytes 12296 | tf_op jit(solution)/shard_map/ppermute | solution.py:38
  9.2 10.3 %collective-permute-start.5 = (f32[1,2,32]{2,1,0:T(2,128)S(1)}, f32[1,2,32]{2,1,0:T(2,128)S(1)}, u32[]{:S(2)}, u32[]{:S(2)}) collective-permute-start(f32[1,2,32]{2,1,0:T(2,128)S(1)} %pad_maximum_fusion.4), channel_id=1, source_target_pairs={{0,16},{4,20},{8,24},{12,28},{16,0},{20,4},{24,8},{28,12},{1,17},{... | collective-permute-start | bytes 776 | tf_op jit(solution)/shard_map/ppermute | solution.py:49
  12.1 10.5 %all-to-all-start = ((bf16[4,2,2048]{2,1,0:T(2,128)(2,1)}), bf16[4,2,2048]{2,1,0:T(2,128)(2,1)S(1)}, u32[]{:S(2)}, u32[]{:S(2)}) async-start(bf16[4,2,2048]{2,1,0:T(2,128)(2,1)} %reshape.430), calls=%async_computation | async-start | bytes 65536 | tf_op jit(solution)/shard_map/all_to_all | solution.py:201
  28.9 7.2 %collective-permute-start.8 = (f32[2,8,256]{2,1,0:T(8,128)S(1)}, f32[2,8,256]{2,1,0:T(8,128)S(1)}, u32[]{:S(2)}, u32[]{:S(2)}) collective-permute-start(f32[2,8,256]{2,1,0:T(8,128)S(1)} %get-tuple-element.101), channel_id=1, source_target_pairs={{0,3},{1,2},{2,1},{3,0},{4,7},{5,6},{6,5},{7,4},{8,11},{9,10},{10,... | collective-permute-start | bytes 49160 | tf_op jit(solution)/shard_map/ppermute | solution.py:26
  36.7 7.9 %collective-permute-start.10 = (f32[1,16,2,32]{3,1,2,0:T(8,128)S(1)}, f32[1,16,2,32]{3,1,2,0:T(8,128)S(1)}, u32[]{:S(2)}, u32[]{:S(2)}) collective-permute-start(f32[1,16,2,32]{3,1,2,0:T(8,128)S(1)} %maximum_bitcast_fusion.1), channel_id=1, source_target_pairs={{4,0},{8,4},{12,8},{16,12},{20,16},{24,20},{28,24},{0,28},{5,1},{9... | collective-permute-start | bytes 12296 | tf_op jit(solution)/shard_map/ppermute | solution.py:40
  36.8 7.8 %collective-permute-start.9 = (f32[1,16,2,32]{3,1,2,0:T(8,128)S(1)}, f32[1,16,2,32]{3,1,2,0:T(8,128)S(1)}, u32[]{:S(2)}, u32[]{:S(2)}) collective-permute-start(f32[1,16,2,32]{3,1,2,0:T(8,128)S(1)} %maximum_bitcast_fusion.1), channel_id=1, source_target_pairs={{0,4},{4,8},{8,12},{12,16},{16,20},{20,24},{24,28},{28,0},{1,5},{5... | collective-permute-start | bytes 12296 | tf_op jit(solution)/shard_map/ppermute | solution.py:38
  37.4 7.1 %collective-permute-start.11 = (f32[16,2,32]{2,1,0:T(2,128)S(1)}, f32[16,2,32]{2,1,0:T(2,128)S(1)}, u32[]{:S(2)}, u32[]{:S(2)}) collective-permute-start(f32[16,2,32]{2,1,0:T(2,128)S(1)} %pad_maximum_fusion.1), channel_id=1, source_target_pairs={{0,16},{4,20},{8,24},{12,28},{16,0},{20,4},{24,8},{28,12},{1,17},{... | collective-permute-start | bytes 12296 | tf_op jit(solution)/shard_map/ppermute | solution.py:49
  41.2 8.9 %all-to-all-start.1 = ((bf16[4,2,2048]{2,1,0:T(2,128)(2,1)}), bf16[4,2,2048]{2,1,0:T(2,128)(2,1)S(1)}, u32[]{:S(2)}, u32[]{:S(2)}) async-start(bf16[4,2,2048]{2,1,0:T(2,128)(2,1)} %reshape.432), calls=%async_computation.1 | async-start | bytes 65536 | tf_op jit(solution)/shard_map/all_to_all | solution.py:201
  55.8 6.9 %collective-permute-start.14 = (f32[2,8,256]{2,1,0:T(8,128)}, f32[2,8,256]{2,1,0:T(8,128)S(1)}, u32[]{:S(2)}, u32[]{:S(2)}) collective-permute-start(f32[2,8,256]{2,1,0:T(8,128)} %get-tuple-element.97), channel_id=1, source_target_pairs={{0,3},{1,2},{2,1},{3,0},{4,7},{5,6},{6,5},{7,4},{8,11},{9,10},{10,... | collective-permute-start | bytes 49160 | tf_op jit(solution)/shard_map/ppermute | solution.py:26
  65.4 7.2 %collective-permute-start.16 = (f32[1,16,2,32]{3,1,2,0:T(8,128)S(1)}, f32[1,16,2,32]{3,1,2,0:T(8,128)S(1)}, u32[]{:S(2)}, u32[]{:S(2)}) collective-permute-start(f32[1,16,2,32]{3,1,2,0:T(8,128)S(1)} %maximum_bitcast_fusion.2), channel_id=1, source_target_pairs={{4,0},{8,4},{12,8},{16,12},{20,16},{24,20},{28,24},{0,28},{5,1},{9... | collective-permute-start | bytes 12296 | tf_op jit(solution)/shard_map/ppermute | solution.py:40
  65.5 6.7 %collective-permute-start.15 = (f32[1,16,2,32]{3,1,2,0:T(8,128)S(1)}, f32[1,16,2,32]{3,1,2,0:T(8,128)S(1)}, u32[]{:S(2)}, u32[]{:S(2)}) collective-permute-start(f32[1,16,2,32]{3,1,2,0:T(8,128)S(1)} %maximum_bitcast_fusion.2), channel_id=1, source_target_pairs={{0,4},{4,8},{8,12},{12,16},{16,20},{20,24},{24,28},{28,0},{1,5},{5... | collective-permute-start | bytes 12296 | tf_op jit(solution)/shard_map/ppermute | solution.py:38
  68.2 9.5 %all-to-all-start.2 = ((bf16[4,2,2048]{2,1,0:T(2,128)(2,1)}), bf16[4,2,2048]{2,1,0:T(2,128)(2,1)S(1)}, u32[]{:S(2)}, u32[]{:S(2)}) async-start(bf16[4,2,2048]{2,1,0:T(2,128)(2,1)} %reshape.434), calls=%async_computation.2 | async-start | bytes 65536 | tf_op jit(solution)/shard_map/all_to_all | solution.py:201
  92.0 9.4 %all-to-all-start.3 = ((bf16[4,2,2048]{2,1,0:T(2,128)(2,1)}), bf16[4,2,2048]{2,1,0:T(2,128)(2,1)S(1)}, u32[]{:S(2)}, u32[]{:S(2)}) async-start(bf16[4,2,2048]{2,1,0:T(2,128)(2,1)} %reshape.436), calls=%async_computation.3 | async-start | bytes 65536 | tf_op jit(solution)/shard_map/all_to_all | solution.py:201
  118.6 9.3 %collective-permute-start.28 = (f32[208,640]{1,0:T(8,128)S(1)}, f32[208,640]{1,0:T(8,128)S(1)}, u32[]{:S(2)}, u32[]{:S(2)}) collective-permute-start(f32[208,640]{1,0:T(8,128)S(1)} %dynamic-slice_bitcast_fusion.1), channel_id=1, source_target_pairs={{0,8},{4,20},{8,0},{12,28},{16,24},{20,4},{24,16},{28,12},{1,9},{5... | collective-permute-start | bytes 1597448 | tf_op jit(solution)/shard_map/ppermute | solution.py:132
  134.6 6.8 %collective-permute-start.30 = (f32[104,640]{1,0:T(8,128)S(1)}, f32[104,640]{1,0:T(8,128)S(1)}, u32[]{:S(2)}, u32[]{:S(2)}) collective-permute-start(f32[104,640]{1,0:T(8,128)S(1)} %bitcast_add_fusion.2), channel_id=1, source_target_pairs={{0,1},{1,0},{2,3},{3,2},{4,5},{5,4},{6,7},{7,6},{8,9},{9,8},{10,11... | collective-permute-start | bytes 798728 | tf_op jit(solution)/shard_map/ppermute | solution.py:132
  141.4 12.5 %collective-permute-start.31 = (f32[104,640]{1,0:T(8,128)S(1)}, f32[104,640]{1,0:T(8,128)S(1)}, u32[]{:S(2)}, u32[]{:S(2)}) collective-permute-start(f32[104,640]{1,0:T(8,128)S(1)} %add.439), channel_id=1, source_target_pairs={{0,2},{1,3},{2,0},{3,1},{4,6},{5,7},{6,4},{7,5},{8,10},{9,11},{10,... | collective-permute-start | bytes 798728 | tf_op jit(solution)/shard_map/ppermute | solution.py:132
  153.9 6.7 %collective-permute-start.32 = (f32[104,640]{1,0:T(8,128)S(1)}, f32[104,640]{1,0:T(8,128)S(1)}, u32[]{:S(2)}, u32[]{:S(2)}) collective-permute-start(f32[104,640]{1,0:T(8,128)S(1)} %add.440), channel_id=1, source_target_pairs={{0,16},{4,12},{8,24},{12,4},{16,0},{20,28},{24,8},{28,20},{1,17},{... | collective-permute-start | bytes 798728 | tf_op jit(solution)/shard_map/ppermute | solution.py:132
  155.5 14.7 %collective-permute-start.21 = (f32[1,16,2,32]{3,1,2,0:T(8,128)S(1)}, f32[1,16,2,32]{3,1,2,0:T(8,128)S(1)}, u32[]{:S(2)}, u32[]{:S(2)}) collective-permute-start(f32[1,16,2,32]{3,1,2,0:T(8,128)S(1)} %maximum_bitcast_fusion.3), channel_id=1, source_target_pairs={{0,4},{4,8},{8,12},{12,16},{16,20},{20,24},{24,28},{28,0},{1,5},{5... | collective-permute-start | bytes 12296 | tf_op jit(solution)/shard_map/ppermute | solution.py:38
  155.5 7.2 %collective-permute-start.22 = (f32[1,16,2,32]{3,1,2,0:T(8,128)S(1)}, f32[1,16,2,32]{3,1,2,0:T(8,128)S(1)}, u32[]{:S(2)}, u32[]{:S(2)}) collective-permute-start(f32[1,16,2,32]{3,1,2,0:T(8,128)S(1)} %maximum_bitcast_fusion.3), channel_id=1, source_target_pairs={{4,0},{8,4},{12,8},{16,12},{20,16},{24,20},{28,24},{0,28},{5,1},{9... | collective-permute-start | bytes 12296 | tf_op jit(solution)/shard_map/ppermute | solution.py:40
  160.6 9.3 %collective-permute-start.33 = (f32[208,640]{1,0:T(8,128)S(1)}, f32[208,640]{1,0:T(8,128)S(1)}, u32[]{:S(2)}, u32[]{:S(2)}) collective-permute-start(f32[208,640]{1,0:T(8,128)S(1)} %bitcast.178), channel_id=1, source_target_pairs={{0,8},{4,20},{8,0},{12,28},{16,24},{20,4},{24,16},{28,12},{1,9},{5... | collective-permute-start | bytes 1597448 | tf_op jit(solution)/shard_map/ppermute | solution.py:132
  170.0 10.7 %collective-permute-start.34 = (f32[416,640]{1,0:T(8,128)S(1)}, f32[416,640]{1,0:T(8,128)S(1)}, u32[]{:S(2)}, u32[]{:S(2)}) collective-permute-start(f32[416,640]{1,0:T(8,128)S(1)} %bitcast.174), channel_id=1, source_target_pairs={{0,4},{4,0},{8,12},{12,8},{16,20},{20,16},{24,28},{28,24},{1,5},{5... | collective-permute-start | bytes 3194888 | tf_op jit(solution)/shard_map/ppermute | solution.py:132
  (46 other events, 263.6 us)
